TPU v7x, 32 devices: a whole 2x2x4 slice. The times are simulated.
32 devices in a mesh: seq: 8 (over z, x), head: 4 (over y, core).
Axes of the slice: x: 2, y: 2, z: 4, core: 2. Of those that a mesh axis runs over, the one named last changes fastest.
Arguments:
- h_in: float32 [2048, 1024], P('seq', 'head'), may hold values from -6 to 6
- norm_gain: float32 [2, 1024], P(None, 'head'), may hold values from 0.5 to 1.5
- w_z: bfloat16 [2, 1024, 2048], P(None, None, 'head'), may hold values from -0.1875 to 0.1875
- w_x: bfloat16 [2, 1024, 2048], P(None, None, 'head'), may hold values from -0.1875 to 0.1875
- w_bc: bfloat16 [2, 1024, 256], replicated, may hold values from -0.1875 to 0.1875
- w_dt: bfloat16 [2, 1024, 32], P(None, None, 'head'), may hold values from -0.1875 to 0.1875
- conv_x_w: float32 [2, 4, 2048], P(None, None, 'head'), may hold values from -3 to 3
- conv_x_b: float32 [2, 2048], P(None, 'head'), may hold values from -0.5 to 0.5
- conv_bc_w: float32 [2, 4, 256], replicated, may hold values from -3 to 3
- conv_bc_b: float32 [2, 256], replicated, may hold values from -0.5 to 0.5
- dt_bias: float32 [2, 32], P(None, 'head'), may hold values from -4 to -1
- a_log: float32 [2, 32], P(None, 'head'), may hold values from -10 to -1
- skip: float32 [2, 32], P(None, 'head'), may hold values from 0.5 to 1.5
- gate_gain: float32 [2, 2048], P(None, 'head'), may hold values from 0.5 to 1.5
- w_out: bfloat16 [2, 2048, 1024], P(None, 'head'), may hold values from -0.125 to 0.125
- d_out: float32 [2048, 1024], P('seq', 'head'), may hold values from -6 to 6
Outputs:
- h_out: float32 [2048, 1024], P('seq', 'head')
- d_h: float32 [2048, 1024], P('seq', 'head')
- d_norm_gain: float32 [2, 1024], P(None, 'head')
- d_w_z: float32 [2, 1024, 2048], P(None, 'seq', 'head')
- d_w_x: float32 [2, 1024, 2048], P(None, 'seq', 'head')
- d_w_bc: float32 [2, 1024, 256], replicated
- d_w_dt: float32 [2, 1024, 32], P(None, 'seq', 'head')
- d_conv_x_w: float32 [2, 4, 2048], P(None, None, 'head')
- d_conv_x_b: float32 [2, 2048], P(None, 'head')
- d_conv_bc_w: float32 [2, 4, 256], replicated
- d_conv_bc_b: float32 [2, 256], replicated
- d_dt_bias: float32 [2, 32], P(None, 'head')
- d_a_log: float32 [2, 32], P(None, 'head')
- d_skip: float32 [2, 32], P(None, 'head')
- d_gate_gain: float32 [2, 2048], P(None, 'head')
- d_w_out: float32 [2, 2048, 1024], P(None, 'head', 'seq')
All inputs are finite; a program needn't handle non-finite values.
Results may differ from a plain program's by a relative error of at most 0.014.
The roundings to bfloat16 on the way count: a program that leaves them out, or rounds other values in their place, can miss the bound.
Values may be sent and summed in bfloat16 or wider, within the bound.
A program may use at most 128 MiB of HBM per device.

v0:
```python
import jax
import jax.numpy as jnp
from jax import lax
from jax.sharding import PartitionSpec as P

D = 1024
HEAD_DIM = 64
STATE = 128
CONV = 4
SPAN = 256
LAYERS = 2
DI = 2048
epsilon = 1e-05
highest = lax.Precision.HIGHEST


def shifted(value, axis, steps):
    count = lax.axis_size(axis)
    first, last = (max(0, -steps), min(count, count - steps))
    return lax.ppermute(value, axis, [(source, source + steps) for source in range(first, last)])


def entering_2(value, axis, join, neutral, backward):
    count, mine = (lax.axis_size(axis), lax.axis_index(axis))
    pieces = jax.tree.map(lambda part: lax.all_gather(part, axis), value)
    if backward:
        pieces = jax.tree.map(lambda part: part[::-1], pieces)
        mine = count - 1 - mine
    total = jax.tree.map(
        lambda part, zero: jnp.full_like(part, 0) + jnp.asarray(zero, part.dtype), value, neutral
    )

    def lap(position, total):
        longer = join(total, jax.tree.map(lambda part: part[position], pieces))
        return jax.tree.map(lambda new, old: jnp.where(position < mine, new, old), longer, total)

    return lax.fori_loop(0, count - 1, lap, total)


def conv_inputs(extended, dt_raw, conv_weight, conv_bias, dt_bias, a_log):
    row_count = dt_raw.shape[0]
    mixed = jnp.zeros((row_count, extended.shape[1]), jnp.float32) + conv_bias[None, :]
    for offset in range(CONV):
        mixed = mixed + conv_weight[offset][None, :] * extended[offset : offset + row_count]
    active = jax.nn.silu(mixed)
    inner = extended.shape[1] - 2 * STATE
    head_count = dt_raw.shape[1]
    values = active[:, :inner].reshape(row_count, head_count, HEAD_DIM)
    b_proj = active[:, inner : inner + STATE]
    c_proj = active[:, inner + STATE :]
    steps_dt = jax.nn.softplus(dt_raw + dt_bias[None, :])
    log_decay = -steps_dt * jnp.exp(a_log)[None, :]
    return (values, b_proj, c_proj, steps_dt, log_decay)


def scan_from_zero(values, b_proj, c_proj, steps_dt, log_decay):
    row_count, head_count = steps_dt.shape
    blocks = row_count // SPAN
    causal = (jnp.arange(SPAN)[:, None] >= jnp.arange(SPAN)[None, :])[None]

    def one_block(carried, block_data):
        block_vals, b_blk, c_blk, dt_blk, la_blk = block_data
        cumulative = jnp.cumsum(la_blk, axis=0)
        cum_heads = cumulative.T
        spread = cum_heads[:, :, None] - cum_heads[:, None, :]
        weights = jnp.where(causal, jnp.exp(jnp.where(causal, spread, 0.0)), 0.0)
        scores = jnp.dot(c_blk, b_blk.T, precision=highest)
        scaled = block_vals * dt_blk[:, :, None]
        y_diag = jnp.einsum("htu,uhp->thp", weights * scores[None], scaled, precision=highest)
        y_off = (
            jnp.einsum("tn,hpn->thp", c_blk, carried, precision=highest)
            * jnp.exp(cumulative)[:, :, None]
        )
        ending = cumulative[-1]
        tail_decay = jnp.exp(ending[None, :] - cumulative)
        updated = carried * jnp.exp(ending)[:, None, None] + jnp.einsum(
            "uhp,un->hpn", scaled * tail_decay[:, :, None], b_blk, precision=highest
        )
        return (updated, y_diag + y_off)

    stacked = (
        values.reshape(blocks, SPAN, head_count, HEAD_DIM),
        b_proj.reshape(blocks, SPAN, STATE),
        c_proj.reshape(blocks, SPAN, STATE),
        steps_dt.reshape(blocks, SPAN, head_count),
        log_decay.reshape(blocks, SPAN, head_count),
    )
    initial = jnp.zeros((head_count, HEAD_DIM, STATE), jnp.float32)
    last_state, outputs = lax.scan(one_block, initial, stacked)
    return (outputs.reshape(row_count, head_count, HEAD_DIM), last_state)


def carry_term(c_proj, log_decay, entering):
    cumulative = jnp.cumsum(log_decay, axis=0)
    return (
        jnp.einsum("tn,hpn->thp", c_proj, entering, precision=highest)
        * jnp.exp(cumulative)[:, :, None]
    )


def link_states(earlier, later):
    return (earlier[0] * later[0], later[0][:, None, None] * earlier[1] + later[1])


def token_sums(partial_sums):
    return lax.psum(partial_sums, "head")


def contract_first(left, right):
    return lax.dot_general(
        left, right, (((0,), (0,)), ((), ())), preferred_element_type=jnp.float32
    )


def local(
    h_in,
    norm_gain,
    w_z,
    w_x,
    w_bc,
    w_dt,
    conv_x_w,
    conv_x_b,
    conv_bc_w,
    conv_bc_b,
    dt_bias,
    a_log,
    skip,
    gate_gain,
    w_out,
    d_out,
):
    row_count = h_in.shape[0]
    inner = w_x.shape[2]
    head_count = w_dt.shape[2]
    hidden = h_in
    kept = []
    for layer_idx in range(LAYERS):
        gain_one = norm_gain[layer_idx]
        full_hidden, full_gain = (
            lax.all_gather(hidden, "head", axis=1, tiled=True),
            lax.all_gather(gain_one, "head", axis=0, tiled=True),
        )
        factor = lax.rsqrt(jnp.mean(full_hidden * full_hidden, axis=1) + epsilon)
        normed = (full_hidden * factor[:, None] * full_gain[None, :]).astype(jnp.bfloat16)
        gate_in = jnp.dot(normed, w_z[layer_idx], preferred_element_type=jnp.float32)
        x_in = jnp.dot(normed, w_x[layer_idx], preferred_element_type=jnp.float32)
        bc_in = jnp.dot(normed, w_bc[layer_idx], preferred_element_type=jnp.float32)
        dt_raw = jnp.dot(normed, w_dt[layer_idx], preferred_element_type=jnp.float32)
        conv_in = jnp.concatenate([x_in, bc_in], axis=1)
        before = shifted(conv_in[row_count - (CONV - 1) :], "seq", 1)
        extended = jnp.concatenate([before, conv_in], axis=0)
        conv_weight = jnp.concatenate([conv_x_w[layer_idx], conv_bc_w[layer_idx]], axis=1)
        conv_bias = jnp.concatenate([conv_x_b[layer_idx], conv_bc_b[layer_idx]], axis=0)
        inputs, input_back = jax.vjp(
            conv_inputs,
            extended,
            dt_raw,
            conv_weight,
            conv_bias,
            dt_bias[layer_idx],
            a_log[layer_idx],
        )
        values, b_proj, c_proj, steps_dt, log_decay = inputs
        local_part, block_back = jax.vjp(
            scan_from_zero, values, b_proj, c_proj, steps_dt, log_decay
        )
        scanned, leaving = local_part
        decays = jnp.exp(jnp.sum(log_decay, axis=0))
        identity = (jnp.ones_like(decays), jnp.zeros_like(leaving))
        entering = entering_2((decays, leaving), "seq", link_states, identity, False)[1]
        carried_part, carry_back = jax.vjp(carry_term, c_proj, log_decay, entering)
        mixed = scanned + carried_part + skip[layer_idx][None, :, None] * values
        gate_act = jax.nn.silu(gate_in)
        gated = mixed.reshape(row_count, inner) * gate_act
        gate_factor = lax.rsqrt(token_sums(jnp.sum(gated * gated, axis=1)) / DI + epsilon)
        scaled = (gated * gate_factor[:, None] * gate_gain[layer_idx][None, :]).astype(jnp.bfloat16)
        out_weight = w_out[layer_idx]
        summed = lax.psum_scatter(
            contract_first(out_weight, scaled.T), "head", scatter_dimension=0, tiled=True
        )
        kept.append(
            (
                hidden,
                factor,
                normed,
                gate_in,
                gate_act,
                gated,
                gate_factor,
                scaled,
                mixed,
                values,
                decays,
                entering,
                input_back,
                block_back,
                carry_back,
            )
        )
        hidden = hidden + summed.T
    grad = d_out
    collected = [None] * LAYERS
    for layer_idx in reversed(range(LAYERS)):
        (
            layer_input,
            factor,
            normed,
            gate_in,
            gate_act,
            gated,
            gate_factor,
            scaled,
            mixed,
            values,
            decays,
            entering,
            input_back,
            block_back,
            carry_back,
        ) = kept[layer_idx]
        grad_b = grad.astype(jnp.bfloat16)
        out_weight = w_out[layer_idx]
        grad_cols = lax.all_gather(grad_b, "head", axis=1, tiled=True)
        d_part = lax.dot_general(
            grad_cols, out_weight, (((1,), (1,)), ((), ())), preferred_element_type=jnp.float32
        )
        d_cols = contract_first(scaled, grad_cols)
        normalized = gated * gate_factor[:, None]
        d_ggain = jnp.sum(d_part * normalized, axis=0)
        d_norm_in = d_part * gate_gain[layer_idx][None, :]
        along = token_sums(jnp.sum(d_norm_in * normalized, axis=1)) / DI
        d_gated = gate_factor[:, None] * (d_norm_in - normalized * along[:, None])
        sigma = jax.nn.sigmoid(gate_in)
        d_gate = d_gated * mixed.reshape(row_count, inner) * sigma * (1.0 + gate_in * (1.0 - sigma))
        d_mixed = (d_gated * gate_act).reshape(row_count, head_count, HEAD_DIM)
        d_skipped = jnp.sum(d_mixed * values, axis=(0, 2))
        d_c_carry, d_la_carry, d_entering = carry_back(d_mixed)
        back_identity = (jnp.ones_like(decays), jnp.zeros_like(d_entering))
        leaving_grad = entering_2((decays, d_entering), "seq", link_states, back_identity, True)[1]
        d_decays = jnp.sum(leaving_grad * entering, axis=(1, 2)) * decays
        d_values, d_b_proj, d_c_local, d_steps, d_la_local = block_back((d_mixed, leaving_grad))
        d_values = d_values + skip[layer_idx][None, :, None] * d_mixed
        d_inputs = (
            d_values,
            d_b_proj,
            d_c_carry + d_c_local,
            d_steps,
            d_la_carry + d_la_local + d_decays[None, :],
        )
        d_extended, d_dtraw, d_cweight, d_cbias, d_dtbias, d_alog = input_back(d_inputs)
        returned = shifted(d_extended[: CONV - 1], "seq", -1)
        d_conv = d_extended[CONV - 1 :] + jnp.pad(returned, ((row_count - (CONV - 1), 0), (0, 0)))
        d_gate_b = d_gate.astype(jnp.bfloat16)
        d_x_b = d_conv[:, :inner].astype(jnp.bfloat16)
        d_shared = d_conv[:, inner:]
        d_dt_b = d_dtraw.astype(jnp.bfloat16)
        d_wz = contract_first(normed, d_gate_b)
        d_wx = contract_first(normed, d_x_b)
        d_wdt = contract_first(normed, d_dt_b)
        d_wbc = lax.dot_general(
            normed.astype(jnp.float32), d_shared, (((0,), (0,)), ((), ())), precision=highest
        )
        wz_now = w_z[layer_idx]
        wx_now = w_x[layer_idx]
        wdt_now = w_dt[layer_idx]
        wbc_now = w_bc[layer_idx]

        def product(weight, grads):
            return lax.dot_general(
                weight, grads, (((1,), (1,)), ((), ())), preferred_element_type=jnp.float32
            )

        shared_rows = wbc_now.astype(jnp.float32)
        shared_term = lax.dot_general(
            shared_rows, d_shared, (((1,), (1,)), ((), ())), precision=highest
        )
        d_normed = lax.psum_scatter(
            product(wz_now, d_gate_b)
            + product(wx_now, d_x_b)
            + product(wdt_now, d_dt_b)
            + shared_term,
            "head",
            scatter_dimension=0,
            tiled=True,
        ).T
        centered = layer_input * factor[:, None]
        d_ngain = jnp.sum(d_normed * centered, axis=0)
        d_unit = d_normed * norm_gain[layer_idx][None, :]
        along_in = token_sums(jnp.sum(d_unit * centered, axis=1)) / D
        grad = grad + factor[:, None] * (d_unit - centered * along_in[:, None])
        collected[layer_idx] = (
            d_wz,
            d_wx,
            d_wdt,
            d_cols,
            d_ngain,
            d_cweight[:, :inner],
            d_cbias[:inner],
            d_ggain,
            d_dtbias,
            d_alog,
            d_skipped,
            d_wbc,
            d_cweight[:, inner:],
            d_cbias[inner:],
        )
    stacks = [
        jnp.stack([collected[layer_idx][member] for layer_idx in range(LAYERS)])
        for member in range(14)
    ]
    weight_sums = (
        lax.psum_scatter(
            stacks[0].astype(jnp.bfloat16), "seq", scatter_dimension=1, tiled=True
        ).astype(jnp.float32),
        lax.psum_scatter(
            stacks[1].astype(jnp.bfloat16), "seq", scatter_dimension=1, tiled=True
        ).astype(jnp.float32),
        lax.psum_scatter(
            stacks[2].astype(jnp.bfloat16), "seq", scatter_dimension=1, tiled=True
        ).astype(jnp.float32),
        lax.psum_scatter(
            stacks[3].astype(jnp.bfloat16), "seq", scatter_dimension=2, tiled=True
        ).astype(jnp.float32),
    )
    vector_sums = lax.psum(
        (stacks[4], stacks[5], stacks[6], stacks[7], stacks[8], stacks[9], stacks[10]), "seq"
    )
    shared_sums = lax.psum((stacks[11], stacks[12], stacks[13]), ("seq", "head"))
    return (
        hidden,
        grad,
        vector_sums[0],
        weight_sums[0],
        weight_sums[1],
        shared_sums[0],
        weight_sums[2],
        vector_sums[1],
        vector_sums[2],
        shared_sums[1],
        shared_sums[2],
        vector_sums[4],
        vector_sums[5],
        vector_sums[6],
        vector_sums[3],
        weight_sums[3],
    )


def solution(mesh):
    return jax.shard_map(
        local,
        mesh=mesh,
        in_specs=(
            P("seq", "head"),
            P(None, "head"),
            P(None, None, "head"),
            P(None, None, "head"),
            P(),
            P(None, None, "head"),
            P(None, None, "head"),
            P(None, "head"),
            P(),
            P(),
            P(None, "head"),
            P(None, "head"),
            P(None, "head"),
            P(None, "head"),
            P(None, "head", None),
            P("seq", "head"),
        ),
        out_specs=(
            P("seq", "head"),
            P("seq", "head"),
            P(None, "head"),
            P(None, "seq", "head"),
            P(None, "seq", "head"),
            P(),
            P(None, "seq", "head"),
            P(None, None, "head"),
            P(None, "head"),
            P(),
            P(),
            P(None, "head"),
            P(None, "head"),
            P(None, "head"),
            P(None, "head"),
            P(None, "head", "seq"),
        ),
        check_vma=False,
    )
```

profile of v0, /device:TPU:0, one launch (start us, length us, event | category | flops | bytes accessed | tf_op | source)
XLA Modules:
  0.0 995.1 jit_solution(10929443034664853142)
XLA Ops:
  8.7 6.0 all-gather
  22.1 6.9 all-gather.15.cloned.1.call-done
  45.5 21.2 %all-reduce.26 = f32[64]{0:T(128)S(1)} all-reduce(f32[64]{0:T(128)S(1)} %exponential_dynamic-update-slice_fusion.1), channel_id=3, replica_groups=mesh['seq'=8,'head'=4] {'seq'}, use_global_device_ids=true, to_apply=%add.26 | all-reduce | flops 64 | bytes 512
  68.5 23.3 %all-gather.19.cloned.1.call-done = f32[64,64,128]{2,1,0:T(8,128)} async-done(((f32[8,64,128]{2,1,0:T(8,128)}), f32[64,64,128]{2,1,0:T(8,128)}) %all-gather.19.cloned.1.call-update) | async-done | bytes 2097168 | tf_op jit(solution)/shard_map/all_gather | solution.py:25
  91.8 7.6 while.44
  109.1 5.8 psum.112
  117.8 23.7 %reduce-scatter.13.cloned.1.call-done = f32[256,256]{0,1:T(8,128)} async-done(((f32[1024,256]{0,1:T(8,128)}), f32[256,256]{0,1:T(8,128)}) %reduce-scatter.13.cloned.1.call-update) | async-done | bytes 262160 | tf_op jit(solution)/shard_map/reduce_scatter | solution.py:179
  149.6 10.6 %all-gather.17.cloned.1.call-done = f32[256,1024]{1,0:T(8,128)} async-done(((f32[256,256]{1,0:T(8,128)}), f32[256,1024]{1,0:T(8,128)}) %all-gather.17.cloned.1.call-update) | async-done | bytes 1048592 | tf_op jit(solution)/shard_map/all_gather | solution.py:141
  181.6 7.0 all_gather.64
  189.3 22.7 %all-reduce.27 = f32[64]{0:T(128)S(1)} all-reduce(f32[64]{0:T(128)S(1)} %exponential_dynamic-update-slice_fusion), channel_id=6, replica_groups=mesh['seq'=8,'head'=4] {'seq'}, use_global_device_ids=true, to_apply=%add.27 | all-reduce | flops 64 | bytes 512
  217.7 13.2 %all-gather.21.cloned.1.call-done = f32[64,64,128]{2,1,0:T(8,128)} async-done(((f32[8,64,128]{2,1,0:T(8,128)}), f32[64,64,128]{2,1,0:T(8,128)}) %all-gather.21.cloned.1.call-update) | async-done | bytes 2097168 | tf_op jit(solution)/shard_map/all_gather | solution.py:25
  230.9 15.9 %while.45 = (s32[]{:T(128)}, f32[8,64,128]{2,1,0:T(8,128)S(1)}, s32[]{:T(128)}, f32[8,8]{1,0:T(8,128)}, f32[8,8,64,128]{3,2,1,0:T(8,128)}, /*index=5*/s32[]{:T(128)}, s32[]{:T(128)}) while((s32[]{:T(128)}, f32[8,64,128]{2,1,0:T(8,128)S(1)}, s32[]{:T(128)}, f32[8,8]{1,0:T(8,128)}, f32[8,8,64,128]{3,2,1,0:T(8,128)}, ...), condition=%wide.region_14.16_spmd.clone, body=%wide.region_13.15_spmd.clone.sunk | while | flops 262148 | bytes 786633 | solution.py:37
  258.1 5.6 psum.113
  267.1 6.6 psum.114
  306.4 22.6 %all-gather.23.cloned.1.call-done = f32[64,64,128]{2,1,0:T(8,128)} async-done(((f32[8,64,128]{2,1,0:T(8,128)}), f32[64,64,128]{2,1,0:T(8,128)}) %all-gather.23.cloned.1.call-update) | async-done | bytes 2097168 | tf_op jit(solution)/shard_map/all_gather | solution.py:25
  332.1 15.8 %while.46 = (s32[]{:T(128)}, f32[8,64,128]{2,1,0:T(8,128)S(1)}, s32[]{:T(128)}, f32[8,8]{1,0:T(8,128)}, f32[8,8,64,128]{3,2,1,0:T(8,128)}, /*index=5*/s32[]{:T(128)}, s32[]{:T(128)}) while((s32[]{:T(128)}, f32[8,64,128]{2,1,0:T(8,128)S(1)}, s32[]{:T(128)}, f32[8,8]{1,0:T(8,128)}, f32[8,8,64,128]{3,2,1,0:T(8,128)}, ...), condition=%wide.region_22.24_spmd.clone, body=%wide.region_21.23_spmd.clone.sunk | while | flops 262148 | bytes 786633 | solution.py:37
  388.6 21.4 %reduce-scatter.17.cloned.1.call-done = f32[256,256]{0,1:T(8,128)} async-done(((f32[1024,256]{0,1:T(8,128)}), f32[256,256]{0,1:T(8,128)}) %reduce-scatter.17.cloned.1.call-update) | async-done | bytes 262160 | tf_op jit(solution)/shard_map/reduce_scatter | solution.py:278
  411.7 5.7 psum.115
  417.5 19.9 %reduce-scatter.15.cloned.1.call-done = f32[256,256]{0,1:T(8,128)} async-done(((f32[1024,256]{0,1:T(8,128)}), f32[256,256]{0,1:T(8,128)}) %reduce-scatter.15.cloned.1.call-update) | async-done | bytes 262160 | tf_op jit(solution)/shard_map/reduce_scatter | solution.py:179
  439.6 6.7 all_gather.67
  449.0 6.7 psum.116
  475.4 35.6 %all-gather.25.cloned.1.call-done = f32[64,64,128]{2,1,0:T(8,128)} async-done(((f32[8,64,128]{2,1,0:T(8,128)}), f32[64,64,128]{2,1,0:T(8,128)}) %all-gather.25.cloned.1.call-update) | async-done | bytes 2097168 | tf_op jit(solution)/shard_map/all_gather | solution.py:25
  514.2 12.3 %while.47 = (s32[]{:T(128)}, f32[8,64,128]{2,1,0:T(8,128)S(1)}, s32[]{:T(128)}, f32[8,8]{1,0:T(8,128)}, f32[8,8,64,128]{3,2,1,0:T(8,128)}, /*index=5*/s32[]{:T(128)}, s32[]{:T(128)}) while((s32[]{:T(128)}, f32[8,64,128]{2,1,0:T(8,128)S(1)}, s32[]{:T(128)}, f32[8,8]{1,0:T(8,128)}, f32[8,8,64,128]{3,2,1,0:T(8,128)}, ...), condition=%wide.region_43.45_spmd.clone, body=%wide.region_42.44_spmd.clone.sunk | while | flops 262148 | bytes 786633 | solution.py:37
  546.2 6.2 copy.152
  597.7 41.8 %all-reduce.28 = (f32[2,4,256]{2,1,0:T(4,128)}, f32[2,256]{1,0:T(2,128)}) all-reduce(f32[2,4,256]{2,1,0:T(4,128)S(1)} %pad_maximum_fusion.8, f32[2,256]{1,0:T(2,128)S(1)} %pad_maximum_fusion.16), channel_id=1, replica_groups=mesh['seq'=8,'head'=4] {'seq','head'}, use_global_device_ids=true, to_apply=%region_79.81 | all-reduce | flops 2560 | bytes 20480 | tf_op jit(solution)/shard_map/psum | solution.py:329
  643.6 31.7 %reduce-scatter.27.cloned.1.call-done = bf16[128,1024]{1,0:T(8,128)(2,1)} async-done(((bf16[1024,1024]{1,0:T(8,128)(2,1)}), bf16[128,1024]{1,0:T(8,128)(2,1)}) %reduce-scatter.27.cloned.1.call-update) | async-done | bytes 262160
  677.5 69.4 %reduce-scatter.21.cloned.1.call-done = bf16[2,128,512]{2,1,0:T(8,128)(2,1)} async-done(((bf16[2,1024,512]{2,1,0:T(8,128)(2,1)}), bf16[2,128,512]{2,1,0:T(8,128)(2,1)}) %reduce-scatter.21.cloned.1.call-update) | async-done | bytes 262160 | tf_op jit(solution)/shard_map/reduce_scatter | solution.py:313
  748.7 24.5 %reduce-scatter.19.cloned.1.call-done = f32[256,256]{0,1:T(8,128)} async-done(((f32[1024,256]{0,1:T(8,128)}), f32[256,256]{0,1:T(8,128)}) %reduce-scatter.19.cloned.1.call-update) | async-done | bytes 262160 | tf_op jit(solution)/shard_map/reduce_scatter | solution.py:278
  774.4 5.8 psum.117
  780.1 38.2 %all-reduce.29 = (f32[2,256]{1,0:T(2,128)}, f32[2,4,512]{2,1,0:T(4,128)}, f32[2,512]{1,0:T(2,128)}, f32[2,8]{1,0:T(2,128)}, f32[2,8]{1,0:T(2,128)}, /*index=5*/f32[2,8]{1,0:T(2,128)}, f32[2,512]{1,0:T(2,128)}) all-reduce(f32[2,256]{1,0:T(2,128)S(1)} %pad_maximum_fusion.15, ...), channel_id=1, replica_groups=mesh['seq'=8,'head'=4] {'seq'}, use_global_device_ids=true, to_apply=%region_62.64 | all-reduce | flops 6704 | bytes 53632 | tf_op jit(solution)/shard_map/psum | solution.py:326
  820.2 25.9 %reduce-scatter.23.cloned.1.call-done = bf16[2,128,512]{2,1,0:T(8,128)(2,1)} async-done(((bf16[2,1024,512]{2,1,0:T(8,128)(2,1)}), bf16[2,128,512]{2,1,0:T(8,128)(2,1)}) %reduce-scatter.23.cloned.1.call-update) | async-done | bytes 262160 | tf_op jit(solution)/shard_map/reduce_scatter | solution.py:316
  847.9 137.2 %all-reduce.32.cloned.1.call-done = f32[2,1024,256]{2,1,0:T(8,128)} async-done(((f32[2,1024,256]{2,1,0:T(8,128)}), f32[2,1024,256]{2,1,0:T(8,128)}) %all-reduce.32.cloned.1.call-update) | async-done | bytes 2097168 | tf_op jit(solution)/shard_map/psum | solution.py:329
  (630 shorter events, 325.7 us)
Async XLA Ops:
  7.2 21.8 %all-gather.15.cloned.1.call-start = ((), (), s32[]{:S(2)}) async-start(), calls=%async_computation.8 | async-start | bytes 1310720 | tf_op jit(solution)/shard_map/all_gather | solution.py:141
  7.9 83.9 %all-gather.19.cloned.1.call-start = ((), (), s32[]{:S(2)}) async-start(), calls=%async_computation.17 | async-start | bytes 2359296 | tf_op jit(solution)/shard_map/all_gather | solution.py:25
  8.7 134.5 %copy-start.103 = (f32[1,256]{1,0:T(1,128)}, f32[1,256]{1,0:T(1,128)S(1)}, u32[]{:S(2)}) copy-start(f32[1,256]{1,0:T(1,128)S(1)} %get-tuple-element.1312) | copy-start | bytes 3076
  32.9 6.0 collective-permute-start
  40.3 59.1 %copy-start = (f32[256,768]{1,0:T(8,128)}, f32[256,768]{1,0:T(8,128)S(1)}, u32[]{:S(2)}) copy-start(f32[256,768]{1,0:T(8,128)S(1)} %get-tuple-element.1275) | copy-start | bytes 2359300
  40.7 59.4 %copy-start.17 = (f32[256,512]{0,1:T(8,128)}, f32[256,512]{0,1:T(8,128)S(1)}, u32[]{:S(2)}) copy-start(f32[256,512]{0,1:T(8,128)S(1)} %copy.129) | copy-start | bytes 1572868
  42.3 99.1 %reduce-scatter.13.cloned.1.call-start = ((), (), s32[]{:S(2)}) async-start(), calls=%async_computation.9 | async-start | bytes 1310720 | tf_op jit(solution)/shard_map/reduce_scatter | solution.py:179
  44.8 55.2 %copy-start.134 = (f32[8]{0:T(128)}, f32[8]{0:T(128)S(1)}, u32[]{:S(2)}) copy-start(f32[8]{0:T(128)S(1)} %get-tuple-element.1317) | copy-start | bytes 100
  45.4 69.5 %copy-start.88 = (f32[1,512]{1,0:T(1,128)}, f32[1,512]{1,0:T(1,128)S(1)}, u32[]{:S(2)}) copy-start(f32[1,512]{1,0:T(1,128)S(1)} %get-tuple-element.1307) | copy-start | bytes 6148
  117.7 42.5 %all-gather.17.cloned.1.call-start = ((), (), s32[]{:S(2)}) async-start(), calls=%async_computation.10 | async-start | bytes 1310720 | tf_op jit(solution)/shard_map/all_gather | solution.py:141
  143.2 87.7 %all-gather.21.cloned.1.call-start = ((), (), s32[]{:S(2)}) async-start(), calls=%async_computation.18 | async-start | bytes 2359296 | tf_op jit(solution)/shard_map/all_gather | solution.py:25
  167.1 4.8 collective-permute-start.1
  180.5 148.4 %all-gather.23.cloned.1.call-start = ((), (), s32[]{:S(2)}) async-start(), calls=%async_computation.19 | async-start | bytes 2359296 | tf_op jit(solution)/shard_map/all_gather | solution.py:25
  281.6 128.5 %reduce-scatter.17.cloned.1.call-start = ((), (), s32[]{:S(2)}) async-start(), calls=%async_computation.12 | async-start | bytes 1310720 | tf_op jit(solution)/shard_map/reduce_scatter | solution.py:278
  376.8 5.6 collective-permute-start.2
  385.7 51.7 %reduce-scatter.15.cloned.1.call-start = ((), (), s32[]{:S(2)}) async-start(), calls=%async_computation.11 | async-start | bytes 1310720 | tf_op jit(solution)/shard_map/reduce_scatter | solution.py:179
  388.5 58.5 %copy-start.23 = (f32[256,512]{1,0:T(8,128)S(1)}, f32[256,512]{1,0:T(8,128)}, u32[]{:S(2)}) copy-start(f32[256,512]{1,0:T(8,128)} %copy-done.22) | copy-start | bytes 1572868
  388.5 58.5 %copy-start.89 = (f32[1,512]{1,0:T(1,128)S(1)}, f32[1,512]{1,0:T(1,128)}, u32[]{:S(2)}) copy-start(f32[1,512]{1,0:T(1,128)} %copy-done.88) | copy-start | bytes 6148
  388.5 58.5 %copy-start.94 = (f32[256]{0:T(256)S(1)}, f32[256]{0:T(256)}, u32[]{:S(2)}) copy-start(f32[256]{0:T(256)} %copy-done.93) | copy-start | bytes 3076
  388.6 122.4 %all-gather.25.cloned.1.call-start = ((), (), s32[]{:S(2)}) async-start(), calls=%async_computation.20 | async-start | bytes 2359296 | tf_op jit(solution)/shard_map/all_gather | solution.py:25
  461.4 180.5 %reduce-scatter.25.cloned.1.call-start = ((), (), s32[]{:S(2)}) async-start(), calls=%async_computation.21 | async-start | bytes 294912
  543.1 132.2 %reduce-scatter.27.cloned.1.call-start = ((), (), s32[]{:S(2)}) async-start(), calls=%async_computation.22 | async-start | bytes 2359296
  555.9 191.0 %reduce-scatter.21.cloned.1.call-start = ((), (), s32[]{:S(2)}) async-start(), calls=%async_computation.14 | async-start | bytes 2359296 | tf_op jit(solution)/shard_map/reduce_scatter | solution.py:313
  560.2 213.0 %reduce-scatter.19.cloned.1.call-start = ((), (), s32[]{:S(2)}) async-start(), calls=%async_computation.13 | async-start | bytes 1310720 | tf_op jit(solution)/shard_map/reduce_scatter | solution.py:278
  583.2 5.9 collective-permute-start.3
  592.1 254.0 %reduce-scatter.23.cloned.1.call-start = ((), (), s32[]{:S(2)}) async-start(), calls=%async_computation.15 | async-start | bytes 2359296 | tf_op jit(solution)/shard_map/reduce_scatter | solution.py:316
  594.8 390.2 %all-reduce.32.cloned.1.call-start = ((), (), s32[]{:S(2)}) async-start(), calls=%async_computation.16 | async-start | bytes 4194304 | tf_op jit(solution)/shard_map/psum | solution.py:329
  641.8 131.4 %copy-start.29 = (f32[256,256]{1,0:T(8,128)S(1)}, f32[256,256]{1,0:T(8,128)}, u32[]{:S(2)}) copy-start(f32[256,256]{1,0:T(8,128)} %param.25) | copy-start | bytes 786436
  641.9 131.4 %copy-start.102 = (f32[1,256]{1,0:T(1,128)S(1)}, f32[1,256]{1,0:T(1,128)}, u32[]{:S(2)}) copy-start(f32[1,256]{1,0:T(1,128)} %copy-done.101) | copy-start | bytes 3076
  641.9 131.4 %copy-start.109 = (f32[256]{0:T(256)S(1)}, f32[256]{0:T(256)}, u32[]{:S(2)}) copy-start(f32[256]{0:T(256)} %copy-done.108) | copy-start | bytes 3076
  641.9 138.2 %copy-start.123 = (f32[256]{0:T(256)S(1)}, f32[256]{0:T(256)}, u32[]{:S(2)}) copy-start(f32[256]{0:T(256)} %get-tuple-element.1182) | copy-start | bytes 3076
  641.9 176.5 %copy-start.55 = (f32[256,256]{1,0:T(8,128)S(1)}, f32[256,256]{1,0:T(8,128)}, u32[]{:S(2)}) copy-start(f32[256,256]{1,0:T(8,128)} %get-tuple-element.1264) | copy-start | bytes 786436
  (130 other events, 1273.8 us)
Sparse Core Ops, SparseCore 0:
  9.5 19.4 all-gather.14
  42.4 49.3 all-gather.18
  117.8 23.5 reduce-scatter.12
  143.4 16.6 all-gather.16
  180.7 50.1 all-gather.20
  281.7 47.2 all-gather.22
  385.8 24.1 reduce-scatter.16
  412.6 24.7 reduce-scatter.14
  461.5 49.4 all-gather.24
  543.2 60.5 reduce-scatter.24
  607.4 67.9 reduce-scatter.26
  679.3 67.6 reduce-scatter.20
  749.5 23.7 reduce-scatter.18
  776.6 69.4 reduce-scatter.22
  851.3 133.7 all-reduce.31
where the time goes:
time: 1010 us; the launch traced here: 995 us
  waiting for transfers between devices  475 us (47%)
  blocking collectives  185 us (18%)
  other arithmetic  110 us (11%)
  matrix products  100 us (10%)
  local copies, waits for them, and re-layouts  96.9 us (10%)
  between operations  17.1 us (2%)
  starting transfers between devices  10.5 us (1%)
    psum x1, waiting for transfers between devices, local(): lax.psum((stacks[11], stacks[12], stacks[13]), ('seq', 'head'))  137 us
    all_gather x4, waiting for transfers between devices, entering_2(): pieces = jax.tree.map(lambda part: lax.all_gather(part, axis), value)  94.6 us
    reduce_scatter x1, waiting for transfers between devices, local(): lax.psum_scatter(stacks[0].astype(jnp.bfloat16), 'seq', scatter_dimension...  69.4 us
    reduce_scatter x2, waiting for transfers between devices, local(): lax.psum_scatter(product(wz_now, d_gate_b) + product(wx_now, d_x_b) + pro...  45.9 us
    unnamed x2, blocking collectives  43.9 us
    reduce_scatter x2, waiting for transfers between devices, local(): lax.psum_scatter(contract_first(out_weight, scaled.T), 'head', scatter_di...  43.6 us
    psum x1, blocking collectives, local(): lax.psum((stacks[11], stacks[12], stacks[13]), ('seq', 'head'))  41.8 us
    psum x1, blocking collectives, local(): lax.psum((stacks[4], stacks[5], stacks[6], stacks[7], stacks[8], stacks[9...  38.2 us
  transfers between devices with their start and end apart: 19, of which 17 were waited for; matrix products, arithmetic and copies ran while one was open for 13% of the time, Pallas kernels for 0%

commit v1 on v0

--- a/solution.py
+++ b/solution.py
@@ -326,7 +326,8 @@
     vector_sums = lax.psum(
         (stacks[4], stacks[5], stacks[6], stacks[7], stacks[8], stacks[9], stacks[10]), "seq"
     )
-    shared_sums = lax.psum((stacks[11], stacks[12], stacks[13]), ("seq", "head"))
+    half = lax.psum((stacks[11], stacks[12], stacks[13]), "seq")
+    shared_sums = lax.psum(half, "head")
     return (
         hidden,
         grad,

time: 1010 us -> 1050 us (1.040)
  waiting for transfers between devices: 475 us -> 546 us
  blocking collectives: 185 us -> 149 us
    unnamed x17 -> x18, waiting for transfers between devices: 32.7 us -> 135 us
    psum x1 -> x0, blocking collectives: 41.8 us -> none  [local(): lax.psum((stacks[11], stacks[12], stacks[13]), ('seq', 'head'))]
    psum x1 -> x2, waiting for transfers between devices: 137 us -> 113 us  [the longest x1 62.1 us: local(): half = lax.psum((stacks[11], stacks[12], stacks[13]), 'seq')]
  transfers between devices with their start and end apart: 19 -> 20, of which waited for: 17 -> 19; matrix products, arithmetic and copies ran while one was open for 13% -> 11% of each run, Pallas kernels for 0% -> 0%
where the time goes in v1:
time: 1050 us; the launch traced here: 1030 us
  waiting for transfers between devices  546 us (52%)
  blocking collectives  149 us (14%)
  other arithmetic  116 us (11%)
  matrix products  103 us (10%)
  local copies, waits for them, and re-layouts  91.8 us (9%)
  between operations  17.1 us (2%)
    unnamed x18, waiting for transfers between devices  135 us
    all_gather x4, waiting for transfers between devices, entering_2(): pieces = jax.tree.map(lambda part: lax.all_gather(part, axis), value)  94.4 us
    reduce_scatter x1, waiting for transfers between devices, local(): lax.psum_scatter(stacks[0].astype(jnp.bfloat16), 'seq', scatter_dimension...  69.4 us
    psum x1, waiting for transfers between devices, local(): half = lax.psum((stacks[11], stacks[12], stacks[13]), 'seq')  62.1 us
    psum x1, waiting for transfers between devices, local(): shared_sums = lax.psum(half, 'head')  50.9 us
    reduce_scatter x2, waiting for transfers between devices, local(): lax.psum_scatter(product(wz_now, d_gate_b) + product(wx_now, d_x_b) + pro...  45.8 us
    unnamed x2, blocking collectives  43.7 us
    reduce_scatter x2, waiting for transfers between devices, local(): lax.psum_scatter(contract_first(out_weight, scaled.T), 'head', scatter_di...  43.6 us
  transfers between devices with their start and end apart: 20, of which 19 were waited for; matrix products, arithmetic and copies ran while one was open for 11% of the time, Pallas kernels for 0%

profile of v1, /device:TPU:0, one launch (start us, length us, event | category | flops | bytes accessed | tf_op | source)
XLA Modules:
  0.0 1033.5 jit_solution(5410172850146453400)
XLA Ops:
  8.7 6.0 all-gather
  22.1 6.9 all-gather.15.cloned.1.call-done
  45.5 21.2 %all-reduce.26 = f32[64]{0:T(128)S(1)} all-reduce(f32[64]{0:T(128)S(1)} %exponential_dynamic-update-slice_fusion.1), channel_id=3, replica_groups=mesh['seq'=8,'head'=4] {'seq'}, use_global_device_ids=true, to_apply=%add.26 | all-reduce | flops 64 | bytes 512
  68.6 23.3 %all-gather.19.cloned.1.call-done = f32[64,64,128]{2,1,0:T(8,128)} async-done(((f32[8,64,128]{2,1,0:T(8,128)}), f32[64,64,128]{2,1,0:T(8,128)}) %all-gather.19.cloned.1.call-update) | async-done | bytes 2097168 | tf_op jit(solution)/shard_map/all_gather | solution.py:25
  91.9 7.6 while.44
  109.3 5.8 psum.133
  117.9 23.7 %reduce-scatter.13.cloned.1.call-done = f32[256,256]{0,1:T(8,128)} async-done(((f32[1024,256]{0,1:T(8,128)}), f32[256,256]{0,1:T(8,128)}) %reduce-scatter.13.cloned.1.call-update) | async-done | bytes 262160 | tf_op jit(solution)/shard_map/reduce_scatter | solution.py:179
  149.7 10.6 %all-gather.17.cloned.1.call-done = f32[256,1024]{1,0:T(8,128)} async-done(((f32[256,256]{1,0:T(8,128)}), f32[256,1024]{1,0:T(8,128)}) %all-gather.17.cloned.1.call-update) | async-done | bytes 1048592 | tf_op jit(solution)/shard_map/all_gather | solution.py:141
  181.8 7.0 all_gather.64
  189.5 22.5 %all-reduce.27 = f32[64]{0:T(128)S(1)} all-reduce(f32[64]{0:T(128)S(1)} %exponential_dynamic-update-slice_fusion), channel_id=6, replica_groups=mesh['seq'=8,'head'=4] {'seq'}, use_global_device_ids=true, to_apply=%add.27 | all-reduce | flops 64 | bytes 512
  217.7 13.3 %all-gather.21.cloned.1.call-done = f32[64,64,128]{2,1,0:T(8,128)} async-done(((f32[8,64,128]{2,1,0:T(8,128)}), f32[64,64,128]{2,1,0:T(8,128)}) %all-gather.21.cloned.1.call-update) | async-done | bytes 2097168 | tf_op jit(solution)/shard_map/all_gather | solution.py:25
  231.1 15.9 %while.45 = (s32[]{:T(128)}, f32[8,64,128]{2,1,0:T(8,128)S(1)}, s32[]{:T(128)}, f32[8,8]{1,0:T(8,128)}, f32[8,8,64,128]{3,2,1,0:T(8,128)}, /*index=5*/s32[]{:T(128)}, s32[]{:T(128)}) while((s32[]{:T(128)}, f32[8,64,128]{2,1,0:T(8,128)S(1)}, s32[]{:T(128)}, f32[8,8]{1,0:T(8,128)}, f32[8,8,64,128]{3,2,1,0:T(8,128)}, ...), condition=%wide.region_14.16_spmd.clone, body=%wide.region_13.15_spmd.clone.sunk | while | flops 262148 | bytes 786633 | solution.py:37
  267.3 6.6 psum.135
  306.6 22.5 %all-gather.23.cloned.1.call-done = f32[64,64,128]{2,1,0:T(8,128)} async-done(((f32[8,64,128]{2,1,0:T(8,128)}), f32[64,64,128]{2,1,0:T(8,128)}) %all-gather.23.cloned.1.call-update) | async-done | bytes 2097168 | tf_op jit(solution)/shard_map/all_gather | solution.py:25
  332.2 15.8 %while.46 = (s32[]{:T(128)}, f32[8,64,128]{2,1,0:T(8,128)S(1)}, s32[]{:T(128)}, f32[8,8]{1,0:T(8,128)}, f32[8,8,64,128]{3,2,1,0:T(8,128)}, /*index=5*/s32[]{:T(128)}, s32[]{:T(128)}) while((s32[]{:T(128)}, f32[8,64,128]{2,1,0:T(8,128)S(1)}, s32[]{:T(128)}, f32[8,8]{1,0:T(8,128)}, f32[8,8,64,128]{3,2,1,0:T(8,128)}, ...), condition=%wide.region_22.24_spmd.clone, body=%wide.region_21.23_spmd.clone.sunk | while | flops 262148 | bytes 786633 | solution.py:37
  359.0 12.3 %reduce-window.90 = f32[8,2,128]{2,0,1:T(8,128)S(1)} reduce-window(f32[8,2,128]{2,0,1:T(8,128)S(1)} %fusion.248, f32[]{:T(128)} %constant.312.clone.1), window={size=1x1x128 pad=0_0x0_0x0_127}, to_apply=%region_33.35 | reduce-window | flops 260096 | bytes 16388 | tf_op jit(solution)/shard_map/reduce-window.24
  398.4 21.4 %reduce-scatter.17.cloned.1.call-done = f32[256,256]{0,1:T(8,128)} async-done(((f32[1024,256]{0,1:T(8,128)}), f32[256,256]{0,1:T(8,128)}) %reduce-scatter.17.cloned.1.call-update) | async-done | bytes 262160 | tf_op jit(solution)/shard_map/reduce_scatter | solution.py:278
  427.2 19.9 %reduce-scatter.15.cloned.1.call-done = f32[256,256]{0,1:T(8,128)} async-done(((f32[1024,256]{0,1:T(8,128)}), f32[256,256]{0,1:T(8,128)}) %reduce-scatter.15.cloned.1.call-update) | async-done | bytes 262160 | tf_op jit(solution)/shard_map/reduce_scatter | solution.py:179
  449.2 6.7 all_gather.67
  459.6 6.7 psum.137
  488.4 35.3 %all-gather.25.cloned.1.call-done = f32[64,64,128]{2,1,0:T(8,128)} async-done(((f32[8,64,128]{2,1,0:T(8,128)}), f32[64,64,128]{2,1,0:T(8,128)}) %all-gather.25.cloned.1.call-update) | async-done | bytes 2097168 | tf_op jit(solution)/shard_map/all_gather | solution.py:25
  526.9 7.8 while.47
  580.9 6.2 copy.152
  603.0 62.1 %all-reduce.33.cloned.1.call-done = f32[2,1024,256]{2,1,0:T(8,128)} async-done(((f32[2,1024,256]{2,1,0:T(8,128)}), f32[2,1024,256]{2,1,0:T(8,128)}) %all-reduce.33.cloned.1.call-update) | async-done | bytes 2097168 | tf_op jit(solution)/shard_map/psum | solution.py:329
  665.2 65.2 %reduce-scatter.25.cloned.1.call-done = bf16[128,16]{1,0:T(8,128)(2,1)} async-done(((bf16[1024,16]{1,0:T(8,128)(2,1)}), bf16[128,16]{1,0:T(8,128)(2,1)}) %reduce-scatter.25.cloned.1.call-update) | async-done | bytes 4112
  731.9 69.3 %reduce-scatter.27.cloned.1.call-done = bf16[128,1024]{1,0:T(8,128)(2,1)} async-done(((bf16[1024,1024]{1,0:T(8,128)(2,1)}), bf16[128,1024]{1,0:T(8,128)(2,1)}) %reduce-scatter.27.cloned.1.call-update) | async-done | bytes 262160
  803.4 69.4 %reduce-scatter.21.cloned.1.call-done = bf16[2,128,512]{2,1,0:T(8,128)(2,1)} async-done(((bf16[2,1024,512]{2,1,0:T(8,128)(2,1)}), bf16[2,128,512]{2,1,0:T(8,128)(2,1)}) %reduce-scatter.21.cloned.1.call-update) | async-done | bytes 262160 | tf_op jit(solution)/shard_map/reduce_scatter | solution.py:313
  874.6 24.4 %reduce-scatter.19.cloned.1.call-done = f32[256,256]{0,1:T(8,128)} async-done(((f32[1024,256]{0,1:T(8,128)}), f32[256,256]{0,1:T(8,128)}) %reduce-scatter.19.cloned.1.call-update) | async-done | bytes 262160 | tf_op jit(solution)/shard_map/reduce_scatter | solution.py:278
  900.2 38.3 %all-reduce.28 = (f32[2,256]{1,0:T(2,128)}, f32[2,4,512]{2,1,0:T(4,128)}, f32[2,512]{1,0:T(2,128)}, f32[2,4,256]{2,1,0:T(4,128)S(1)}, f32[2,256]{1,0:T(2,128)S(1...) all-reduce(f32[2,256]{1,0:T(2,128)S(1)} %get-tuple-element.1335, ...), channel_id=1, replica_groups=mesh['seq'=8,'head'=4] {'seq'}, use_global_device_ids=true, to_apply=%region_62.64 | all-reduce | flops 9264 | bytes 74112 | tf_op jit(solution)/shard_map/psum | solution.py:326
  938.5 11.4 %all-reduce.29 = (f32[256]{0:T(256)S(1)}, f32[2,4,256]{2,1,0:T(4,128)}, f32[2,256]{1,0:T(2,128)}) all-reduce(f32[256]{0:T(256)S(1)} %get-tuple-element.1181, f32[2,4,256]{2,1,0:T(4,128)S(1)} %get-tuple-element.1247, f32[2,256]{1,0:T(2,128)S(1)} %get-tuple-element.1248), channel_id=1, replica_groups=mesh['seq'=8,'head'=4] {'head'}, use_global_device_ids=true, to_apply=%region_59.61 | all-reduce | flops 2816 | bytes 22528 | tf_op jit(solution)/shard_map/psum | solution.py:106
  951.7 19.1 %reduce-scatter.23.cloned.1.call-done = bf16[2,128,512]{2,1,0:T(8,128)(2,1)} async-done(((bf16[2,1024,512]{2,1,0:T(8,128)(2,1)}), bf16[2,128,512]{2,1,0:T(8,128)(2,1)}) %reduce-scatter.23.cloned.1.call-update) | async-done | bytes 262160 | tf_op jit(solution)/shard_map/reduce_scatter | solution.py:316
  972.6 50.9 %all-reduce.35.cloned.1.call-done = f32[2,1024,256]{2,1,0:T(8,128)} async-done(((f32[2,1024,256]{2,1,0:T(8,128)}), f32[2,1024,256]{2,1,0:T(8,128)}) %all-reduce.35.cloned.1.call-update) | async-done | bytes 2097168 | tf_op jit(solution)/shard_map/psum | solution.py:330
  (631 shorter events, 327.7 us)
Async XLA Ops:
  7.2 21.8 %all-gather.15.cloned.1.call-start = ((), (), s32[]{:S(2)}) async-start(), calls=%async_computation.8 | async-start | bytes 1310720 | tf_op jit(solution)/shard_map/all_gather | solution.py:141
  7.9 84.0 %all-gather.19.cloned.1.call-start = ((), (), s32[]{:S(2)}) async-start(), calls=%async_computation.18 | async-start | bytes 2359296 | tf_op jit(solution)/shard_map/all_gather | solution.py:25
  8.7 134.6 %copy-start.99 = (f32[1,256]{1,0:T(1,128)}, f32[1,256]{1,0:T(1,128)S(1)}, u32[]{:S(2)}) copy-start(f32[1,256]{1,0:T(1,128)S(1)} %get-tuple-element.1315) | copy-start | bytes 3076
  32.9 6.1 collective-permute-start
  40.4 59.1 %copy-start = (f32[256,768]{1,0:T(8,128)}, f32[256,768]{1,0:T(8,128)S(1)}, u32[]{:S(2)}) copy-start(f32[256,768]{1,0:T(8,128)S(1)} %get-tuple-element.1278) | copy-start | bytes 2359300
  40.7 59.4 %copy-start.17 = (f32[256,512]{0,1:T(8,128)}, f32[256,512]{0,1:T(8,128)S(1)}, u32[]{:S(2)}) copy-start(f32[256,512]{0,1:T(8,128)S(1)} %copy.129) | copy-start | bytes 1572868
  42.4 99.2 %reduce-scatter.13.cloned.1.call-start = ((), (), s32[]{:S(2)}) async-start(), calls=%async_computation.9 | async-start | bytes 1310720 | tf_op jit(solution)/shard_map/reduce_scatter | solution.py:179
  44.9 55.3 %copy-start.133 = (f32[8]{0:T(128)}, f32[8]{0:T(128)S(1)}, u32[]{:S(2)}) copy-start(f32[8]{0:T(128)S(1)} %get-tuple-element.1320) | copy-start | bytes 100
  45.5 69.6 %copy-start.84 = (f32[1,512]{1,0:T(1,128)}, f32[1,512]{1,0:T(1,128)S(1)}, u32[]{:S(2)}) copy-start(f32[1,512]{1,0:T(1,128)S(1)} %get-tuple-element.1310) | copy-start | bytes 6148
  117.8 42.5 %all-gather.17.cloned.1.call-start = ((), (), s32[]{:S(2)}) async-start(), calls=%async_computation.10 | async-start | bytes 1310720 | tf_op jit(solution)/shard_map/all_gather | solution.py:141
  143.3 87.7 %all-gather.21.cloned.1.call-start = ((), (), s32[]{:S(2)}) async-start(), calls=%async_computation.19 | async-start | bytes 2359296 | tf_op jit(solution)/shard_map/all_gather | solution.py:25
  167.2 4.8 collective-permute-start.1
  180.7 148.3 %all-gather.23.cloned.1.call-start = ((), (), s32[]{:S(2)}) async-start(), calls=%async_computation.20 | async-start | bytes 2359296 | tf_op jit(solution)/shard_map/all_gather | solution.py:25
  281.8 138.0 %reduce-scatter.17.cloned.1.call-start = ((), (), s32[]{:S(2)}) async-start(), calls=%async_computation.12 | async-start | bytes 1310720 | tf_op jit(solution)/shard_map/reduce_scatter | solution.py:278
  386.6 5.6 collective-permute-start.2
  395.5 51.7 %reduce-scatter.15.cloned.1.call-start = ((), (), s32[]{:S(2)}) async-start(), calls=%async_computation.11 | async-start | bytes 1310720 | tf_op jit(solution)/shard_map/reduce_scatter | solution.py:179
  398.3 58.4 %copy-start.85 = (f32[1,512]{1,0:T(1,128)S(1)}, f32[1,512]{1,0:T(1,128)}, u32[]{:S(2)}) copy-start(f32[1,512]{1,0:T(1,128)} %copy-done.84) | copy-start | bytes 6148
  398.3 58.4 %copy-start.90 = (f32[256]{0:T(256)S(1)}, f32[256]{0:T(256)}, u32[]{:S(2)}) copy-start(f32[256]{0:T(256)} %copy-done.89) | copy-start | bytes 3076
  398.4 125.3 %all-gather.25.cloned.1.call-start = ((), (), s32[]{:S(2)}) async-start(), calls=%async_computation.21 | async-start | bytes 2359296 | tf_op jit(solution)/shard_map/all_gather | solution.py:25
  474.1 191.0 %all-reduce.33.cloned.1.call-start = ((), (), s32[]{:S(2)}) async-start(), calls=%async_computation.16 | async-start | bytes 4194304 | tf_op jit(solution)/shard_map/psum | solution.py:329
  555.3 5.6 collective-permute-start.3
  563.3 167.1 %reduce-scatter.25.cloned.1.call-start = ((), (), s32[]{:S(2)}) async-start(), calls=%async_computation.22 | async-start | bytes 294912
  577.8 223.3 %reduce-scatter.27.cloned.1.call-start = ((), (), s32[]{:S(2)}) async-start(), calls=%async_computation.23 | async-start | bytes 2359296
  590.6 282.2 %reduce-scatter.21.cloned.1.call-start = ((), (), s32[]{:S(2)}) async-start(), calls=%async_computation.14 | async-start | bytes 2359296 | tf_op jit(solution)/shard_map/reduce_scatter | solution.py:313
  594.0 305.0 %reduce-scatter.19.cloned.1.call-start = ((), (), s32[]{:S(2)}) async-start(), calls=%async_computation.13 | async-start | bytes 1310720 | tf_op jit(solution)/shard_map/reduce_scatter | solution.py:278
  599.0 371.9 %reduce-scatter.23.cloned.1.call-start = ((), (), s32[]{:S(2)}) async-start(), calls=%async_computation.15 | async-start | bytes 2359296 | tf_op jit(solution)/shard_map/reduce_scatter | solution.py:316
  601.7 421.8 %all-reduce.35.cloned.1.call-start = ((), (), s32[]{:S(2)}) async-start(), calls=%async_computation.17 | async-start | bytes 4194304 | tf_op jit(solution)/shard_map/psum | solution.py:330
  665.1 233.9 %copy-start.27 = (f32[256,256]{1,0:T(8,128)S(1)}, f32[256,256]{1,0:T(8,128)}, u32[]{:S(2)}) copy-start(f32[256,256]{1,0:T(8,128)} %param.25) | copy-start | bytes 786436
  665.1 233.9 %copy-start.98 = (f32[1,256]{1,0:T(1,128)S(1)}, f32[1,256]{1,0:T(1,128)}, u32[]{:S(2)}) copy-start(f32[1,256]{1,0:T(1,128)} %copy-done.97) | copy-start | bytes 3076
  665.1 233.9 %copy-start.105 = (f32[256]{0:T(256)S(1)}, f32[256]{0:T(256)}, u32[]{:S(2)}) copy-start(f32[256]{0:T(256)} %copy-done.104) | copy-start | bytes 3076
  665.1 235.0 %copy-start.124 = (f32[256]{0:T(256)S(1)}, f32[256]{0:T(256)}, u32[]{:S(2)}) copy-start(f32[256]{0:T(256)} %get-tuple-element.1182) | copy-start | bytes 3076
  665.1 284.8 %copy-start.51 = (f32[256,256]{1,0:T(8,128)S(1)}, f32[256,256]{1,0:T(8,128)}, u32[]{:S(2)}) copy-start(f32[256,256]{1,0:T(8,128)} %get-tuple-element.1267) | copy-start | bytes 786436
  (131 other events, 1031.3 us)
Sparse Core Ops, SparseCore 0:
  9.5 19.4 all-gather.14
  42.5 49.3 all-gather.18
  118.0 23.5 reduce-scatter.12
  143.6 16.6 all-gather.16
  180.8 50.1 all-gather.20
  281.9 47.0 all-gather.22
  395.5 24.2 reduce-scatter.16
  422.3 24.7 reduce-scatter.14
  474.2 49.4 all-gather.24
  563.3 101.7 all-reduce.32
  669.0 61.3 reduce-scatter.24
  733.8 67.3 reduce-scatter.26
  805.3 67.4 reduce-scatter.20
  875.2 23.7 reduce-scatter.18
  902.4 68.4 reduce-scatter.22
  973.1 50.3 all-reduce.34
